TPU v7x, 256 devices: a whole 4x4x8 slice. The times are simulated.
256 devices in a mesh: dp: 4 (over y), expert: 64 (over z, x, core).
Axes of the slice: x: 4, y: 4, z: 8, core: 2. Of those that a mesh axis runs over, the one named last changes fastest.
Arguments:
- tokens: bfloat16 [8192, 3584], P('expert', 'dp'), may hold values from -6 to 6
- expert_ids: int32 [8192, 8], P('expert'), may hold values from 0 to 63, as said below
- replica_choice: int32 [8192, 8], P('expert'), may hold values from 0 to 1, as said below
- gate_weights: float32 [8192, 8], P('expert'), may hold values from 0.1 to 1
- placement: int32 [32, 2], replicated, may hold values from 0 to 63, as said below
- capacity: int32 [96], replicated, may hold values from 6 to 12, as said below
- w_gate: bfloat16 [64, 2, 3584, 1024], P('expert', None, 'dp'), as said below
- w_up: bfloat16 [64, 2, 3584, 1024], P('expert', None, 'dp'), as said below
- w_down: bfloat16 [64, 2, 1024, 3584], P('expert', None, None, 'dp'), as said below
Outputs:
- combined: bfloat16 [8192, 3584], P('expert', 'dp')
Inputs may be any that keep to these rules, and one draw needn't show every extreme that they name: `expert_ids`: each row names 8 different experts; in every aligned block of 128 rows some hot expert is named by at least 24 rows. `replica_choice`: 1 only where the slot's expert is hot; in every aligned block of 128 rows both replicas of some hot expert whose replicas have capacity 12 receive 12 or more slots. `placement`: column 0 holds 32 different expert numbers; column 1 holds 32 different expert-axis indices, none of them the own index of a hot expert. Entry e below 64 belongs to expert e's own replica, entry 64 + j to the copy of expert placement[j, 0]; both replicas of some hot expert have capacity 12. w_gate[placement[j, 1], 1] equals w_gate[placement[j, 0], 0]; entry [h, 1] is zero where index h hosts no copy. `w_up`: laid out as w_gate. `w_down`: laid out as w_gate.
All inputs are finite; a program needn't handle non-finite values.
Results may differ from a plain program's by a relative error of at most 0.0057.
Values may be sent and summed in bfloat16 or wider, within the bound.
A program may use at most 128 MiB of HBM per device.

v0:
```python
import jax
import jax.numpy as jnp
from jax import lax
from jax.sharding import PartitionSpec as P


def slot_room(token_count, top_count, expert_count):
    return max(2, min(token_count // 4, 3 * token_count * top_count // (4 * expert_count)))


def on_device(
    tokens, expert_ids, replica_choice, gate_weights, placement, capacity, w_gate, w_up, w_down
):
    expert_count = lax.axis_size("expert")
    token_count, columns = tokens.shape
    top_count = expert_ids.shape[1]
    hot_count = placement.shape[0]
    replicas = expert_count + hot_count
    room_each = slot_room(token_count, top_count, expert_count)
    buffer_slots = expert_count * 2 * room_each
    slot_count = token_count * top_count
    hot_ids = placement[:, 0]
    flat_ids = expert_ids.reshape(-1)
    copy_flag = replica_choice.reshape(-1)
    hot_match = (flat_ids[:, None] == hot_ids[None, :]).astype(jnp.int32)
    hot_slot = jnp.sum(hot_match * jnp.arange(hot_count, dtype=jnp.int32)[None, :], 1)
    target = jnp.where(copy_flag == 1, expert_count + hot_slot, flat_ids)
    onehot = (target[:, None] == jnp.arange(replicas, dtype=jnp.int32)[None, :]).astype(jnp.int32)
    slots = jnp.arange(slot_count, dtype=jnp.int32)
    earlier = (slots[None, :] < slots[:, None]).astype(jnp.bfloat16)
    before = jnp.dot(
        earlier, onehot.astype(jnp.bfloat16), preferred_element_type=jnp.float32
    ).astype(jnp.int32)
    slot_rank = jnp.sum(before * onehot, 1)
    slot_limit = jnp.sum(onehot * capacity[None, :], 1)
    retained = slot_rank < slot_limit
    own_gate = w_gate[0, 0]
    own_up = w_up[0, 0]
    own_down = w_down[0, 0]
    position = jnp.where(retained, (flat_ids * 2 + copy_flag) * room_each + slot_rank, buffer_slots)
    source = jnp.full((buffer_slots,), slot_count, jnp.int32)
    source = source.at[position].set(jnp.arange(slot_count, dtype=jnp.int32), mode="drop")
    filled = source < slot_count
    token_rows = tokens[jnp.minimum(source, slot_count - 1) // top_count]
    outgoing = jnp.where(filled[:, None], token_rows, jnp.zeros((), tokens.dtype)).reshape(
        expert_count, 2, room_each, columns
    )
    received = lax.all_to_all(outgoing, "expert", split_axis=0, concat_axis=0, tiled=True)
    gate_part = jnp.einsum("nkcd,df->nkcf", received, own_gate, preferred_element_type=jnp.float32)
    up_part = jnp.einsum("nkcd,df->nkcf", received, own_up, preferred_element_type=jnp.float32)
    gate_part, up_part = (
        lax.psum_scatter(gate_part, "dp", scatter_dimension=3, tiled=True),
        lax.psum_scatter(up_part, "dp", scatter_dimension=3, tiled=True),
    )
    hidden = (jax.nn.silu(gate_part) * up_part).astype(jnp.bfloat16)
    hidden = lax.all_gather(hidden, "dp", axis=3, tiled=True)
    result = jnp.einsum("nkcf,fd->nkcd", hidden, own_down, preferred_element_type=jnp.float32)
    result = result.astype(jnp.bfloat16)
    returned = lax.all_to_all(result, "expert", split_axis=0, concat_axis=0, tiled=True)
    returned_flat = returned.reshape(buffer_slots, columns)
    picked = returned_flat[jnp.minimum(position, buffer_slots - 1)]
    weight = jnp.where(retained, gate_weights.reshape(-1), jnp.zeros((), jnp.float32))
    combined = jnp.sum(
        (weight[:, None] * picked.astype(jnp.float32)).reshape(token_count, top_count, columns), 1
    )
    return combined.astype(jnp.bfloat16)


def solution(mesh):
    return jax.shard_map(
        on_device,
        mesh=mesh,
        in_specs=(
            P("expert", "dp"),
            P("expert", None),
            P("expert", None),
            P("expert", None),
            P(),
            P(),
            P("expert", None, "dp", None),
            P("expert", None, "dp", None),
            P("expert", None, None, "dp"),
        ),
        out_specs=P("expert", "dp"),
        check_vma=False,
    )
```

profile of v0, /device:TPU:2, one launch (start us, length us, event | category | flops | bytes accessed | tf_op | source)
XLA Modules:
  0.0 399.8 jit_solution(2275369695422325226)
XLA Ops:
  6.5 0.8 copy.35
  7.4 0.7 broadcast_compare_fusion.1
  8.1 0.7 add_multiply_fusion
  10.5 0.8 select_reduce_fusion
  11.5 4.3 %scatter_custom_fusion = s32[1536]{0:T(1024)S(1)} fusion(s32[1024]{0:T(1024)S(1)} %bitcast.34, s32[1024]{0:T(1024)S(1)} %iota.18, s32[]{:T(128)} %constant.20.clone.1), kind=kCustom, calls=%fused_computation.43 | custom fusion | bytes 6148 | tf_op jit(solution)/shard_map/scatter | solution.py:42
  15.9 5.1 %gather_fusion = bf16[1536,896]{1,0:T(8,128)(2,1)S(1)} fusion(bf16[128,896]{1,0:T(8,128)(2,1)S(1)} %copy-done, s32[2048]{0:T(1024)S(1)} %pad_clamp_fusion), kind=kCustom, calls=%fused_computation | custom fusion | bytes 5511168 | tf_op jit(solution)/shard_map/gather | solution.py:44
  21.0 2.5 gather.9
  23.6 2.4 broadcast_select_fusion
  26.0 2.2 copy.38
  28.2 77.4 %all_to_all.10 = bf16[64,2,12,896]{3,1,2,0:T(2,128)(2,1)S(1)} all-to-all(bf16[64,2,12,896]{3,1,2,0:T(2,128)(2,1)S(1)} %copy.38), channel_id=1, replica_groups=mesh['dp'=4,'expert'=64] {'expert'}, dimensions={0} | all-to-all | bytes 5505024 | tf_op jit(solution)/shard_map/all_to_all | solution.py:48
  105.6 5.3 %fusion.4 = f32[64,2,12,1024]{3,0,2,1:T(8,128)} fusion(bf16[64,2,12,896]{3,1,2,0:T(2,128)(2,1)S(1)} %all_to_all.10, bf16[1,2,896,1024]{3,2,1,0:T(8,128)(2,1)S(1)} %copy-done.2), kind=kOutput, calls=%fused_computation.10 | convolution fusion | flops 2818572288 | bytes 10878976 | tf_op jit(solution)/shard_map/nkcd,df->nkcf/dot_general | solution.py:49
  110.9 6.8 %fusion.2 = f32[64,2,12,1024]{3,0,2,1:T(8,128)} fusion(bf16[64,2,12,896]{3,1,2,0:T(2,128)(2,1)S(1)} %all_to_all.10, bf16[1,2,896,1024]{3,2,1,0:T(8,128)(2,1)} %param.16), kind=kOutput, calls=%fused_computation.8 | convolution fusion | flops 2818572288 | bytes 10878976 | tf_op jit(solution)/shard_map/nkcd,df->nkcf/dot_general | solution.py:50
  118.0 56.4 %reduce-scatter.3.cloned.1.call-done = f32[64,2,12,256]{3,0,2,1:T(8,128)} async-done(((f32[64,2,12,1024]{3,0,2,1:T(8,128)}), f32[64,2,12,256]{3,0,2,1:T(8,128)}) %reduce-scatter.3.cloned.1.call-update) | async-done | bytes 1572880 | tf_op jit(solution)/shard_map/reduce_scatter | solution.py:52
  174.3 68.9 %reduce-scatter.5.cloned.1.call-done = f32[64,2,12,256]{3,0,2,1:T(8,128)} async-done(((f32[64,2,12,1024]{3,0,2,1:T(8,128)}), f32[64,2,12,256]{3,0,2,1:T(8,128)}) %reduce-scatter.5.cloned.1.call-update) | async-done | bytes 1572880 | tf_op jit(solution)/shard_map/reduce_scatter | solution.py:53
  243.2 3.3 multiply_convert_fusion
  246.5 45.6 %all-gather.2.cloned.1.call-done = bf16[64,2,12,1024]{3,0,2,1:T(8,128)(2,1)} async-done(((bf16[64,2,12,256]{3,0,2,1:T(8,128)(2,1)}), bf16[64,2,12,1024]{3,0,2,1:T(8,128)(2,1)}) %all-gather.2.cloned.1.call-update) | async-done | bytes 3145744 | tf_op jit(solution)/shard_map/all_gather | solution.py:56
  292.1 5.9 %convolution_convert_fusion = bf16[64,2,12,896]{3,0,2,1:T(8,128)(2,1)S(1)} fusion(bf16[64,2,12,1024]{3,0,2,1:T(8,128)(2,1)} %all-gather.2.cloned.1.call-done, bf16[1,2,1024,896]{3,2,1,0:T(8,128)(2,1)} %param.17), kind=kOutput, calls=%fused_computation.12 | convolution fusion | flops 2819948544 | bytes 7733248 | tf_op jit(solution)/shard_map/nkcf,fd->nkcd/dot_general | solution.py:57
  298.0 4.4 %copy.41 = bf16[64,2,12,896]{3,1,2,0:T(2,128)(2,1)} copy(bf16[64,2,12,896]{3,0,2,1:T(8,128)(2,1)S(1)} %convolution_convert_fusion) | data formatting | bytes 5505024 | tf_op jit(solution)/shard_map/convert_element_type | solution.py:58
  302.4 10.7 %all-to-all-start.1 = ((bf16[64,2,12,896]{3,1,2,0:T(2,128)(2,1)}), bf16[64,2,12,896]{3,1,2,0:T(2,128)(2,1)S(1)}, u32[]{:S(2)}, u32[]{:S(2)}) async-start(bf16[64,2,12,896]{3,1,2,0:T(2,128)(2,1)} %copy.41), calls=%async_computation.3 | async-start | bytes 5505024 | tf_op jit(solution)/shard_map/all_to_all | solution.py:59
  313.4 65.1 %all-to-all-done.1 = bf16[64,2,12,896]{3,1,2,0:T(2,128)(2,1)S(1)} async-done(((bf16[64,2,12,896]{3,1,2,0:T(2,128)(2,1)}), bf16[64,2,12,896]{3,1,2,0:T(2,128)(2,1)S(1)}, u32[]{:S(2)}, u32[]{:S(2)}) %all-to-all-start.1) | async-done | bytes 2752544 | tf_op jit(solution)/shard_map/all_to_all | solution.py:59
  378.4 2.4 copy.42
  380.9 3.8 reshape.134
  384.7 5.3 %gather_fusion.1 = bf16[1024,896]{1,0:T(8,128)(2,1)} fusion(bf16[1536,896]{1,0:T(8,128)(2,1)S(1)} %reshape.134, s32[1024]{0:T(1024)S(1)} %broadcast_clamp_fusion), kind=kCustom, calls=%fused_computation.1 | custom fusion | bytes 3674112 | tf_op jit(solution)/shard_map/gather | solution.py:61
  389.9 3.4 fusion.1
  (33 shorter events, 2.6 us)
Async XLA Ops:
  6.5 9.3 %copy-start = (bf16[128,896]{1,0:T(8,128)(2,1)S(1)}, bf16[128,896]{1,0:T(8,128)(2,1)}, u32[]{:S(2)}) copy-start(bf16[128,896]{1,0:T(8,128)(2,1)} %param.9) | copy-start | bytes 688132
  6.5 167.8 %reduce-scatter.3.cloned.1.call-start = ((), (), s32[]{:S(2)}) async-start(), calls=%async_computation.4 | async-start | bytes 7864320 | tf_op jit(solution)/shard_map/reduce_scatter | solution.py:52
  28.2 77.4 %copy-start.2 = (bf16[1,2,896,1024]{3,2,1,0:T(8,128)(2,1)S(1)}, bf16[1,2,896,1024]{3,2,1,0:T(8,128)(2,1)}, u32[]{:S(2)}) copy-start(bf16[1,2,896,1024]{3,2,1,0:T(8,128)(2,1)} %param.15) | copy-start | bytes 11010052
  110.9 132.3 %reduce-scatter.5.cloned.1.call-start = ((), (), s32[]{:S(2)}) async-start(), calls=%async_computation.5 | async-start | bytes 7864320 | tf_op jit(solution)/shard_map/reduce_scatter | solution.py:53
  117.7 174.4 %all-gather.2.cloned.1.call-start = ((), (), s32[]{:S(2)}) async-start(), calls=%async_computation.6 | async-start | bytes 3932160 | tf_op jit(solution)/shard_map/all_gather | solution.py:56
  302.4 10.8 %copy-start.1 = (f32[128,8]{0,1:T(8,128)S(1)}, f32[128,8]{0,1:T(8,128)}, u32[]{:S(2)}) copy-start(f32[128,8]{0,1:T(8,128)} %param.12) | copy-start | bytes 12292
  302.4 76.0 %all-to-all-start.1 = ((bf16[64,2,12,896]{3,1,2,0:T(2,128)(2,1)}), bf16[64,2,12,896]{3,1,2,0:T(2,128)(2,1)S(1)}, u32[]{:S(2)}, u32[]{:S(2)}) async-start(bf16[64,2,12,896]{3,1,2,0:T(2,128)(2,1)} %copy.41), calls=%async_computation.3 | async-start | bytes 5505024 | tf_op jit(solution)/shard_map/all_to_all | solution.py:59
Sparse Core Ops, SparseCore 0:
  111.0 63.3 reduce-scatter.2
  176.9 66.2 reduce-scatter.4
  246.6 45.4 all-gather.1
where the time goes:
time: 400 us
  waiting for transfers between devices  236 us (59%)
  blocking collectives  77.4 us (19%)
  local copies, waits for them, and re-layouts  32.4 us (8%)
  matrix products  18.5 us (5%)
  between operations  13.3 us (3%)
  other arithmetic  11.3 us (3%)
  starting transfers between devices  10.9 us (3%)
    all_to_all x1, blocking collectives, on_device(): lax.all_to_all(outgoing, 'expert', split_axis=0, concat_axis=0, tiled=True)  77.4 us
    reduce_scatter x1, waiting for transfers between devices, on_device(): lax.psum_scatter(up_part, 'dp', scatter_dimension=3, tiled=True)  68.9 us
    all_to_all x1, waiting for transfers between devices, on_device(): lax.all_to_all(result, 'expert', split_axis=0, concat_axis=0, tiled=True)  65.1 us
    reduce_scatter x1, waiting for transfers between devices, on_device(): lax.psum_scatter(gate_part, 'dp', scatter_dimension=3, tiled=True)  56.4 us
    all_gather x1, waiting for transfers between devices, on_device(): hidden = lax.all_gather(hidden, 'dp', axis=3, tiled=True)  45.6 us
    all_to_all x1, starting transfers between devices, on_device(): lax.all_to_all(result, 'expert', split_axis=0, concat_axis=0, tiled=True)  10.7 us
  transfers between devices with their start and end apart: 4, of which 4 were waited for; matrix products, arithmetic and copies ran while one was open for 2% of the time, Pallas kernels for 0%

commit v1 on v0

--- a/solution.py
+++ b/solution.py
@@ -53,7 +53,9 @@
         lax.psum_scatter(up_part, "dp", scatter_dimension=3, tiled=True),
     )
     hidden = (jax.nn.silu(gate_part) * up_part).astype(jnp.bfloat16)
-    hidden = lax.all_gather(hidden, "dp", axis=3, tiled=True)
+    hidden = jnp.concatenate(
+        lax.all_to_all(jnp.stack([hidden] * lax.axis_size("dp")), "dp", 0, 0), axis=3
+    )
     result = jnp.einsum("nkcf,fd->nkcd", hidden, own_down, preferred_element_type=jnp.float32)
     result = result.astype(jnp.bfloat16)
     returned = lax.all_to_all(result, "expert", split_axis=0, concat_axis=0, tiled=True)

time: 400 us -> 395 us (0.988)
  waiting for transfers between devices: 236 us -> 191 us
  blocking collectives: 77.4 us -> 118 us
    all_gather x1 -> x0, waiting for transfers between devices: 45.6 us -> none  [on_device(): hidden = lax.all_gather(hidden, 'dp', axis=3, tiled=True)]
    all_to_all x0 -> x1, blocking collectives: none -> 40.4 us  [on_device(): lax.all_to_all(jnp.stack([hidden] * lax.axis_size('dp')), 'dp', 0, 0)]
  transfers between devices with their start and end apart: 4 -> 3, of which waited for: 4 -> 3; matrix products, arithmetic and copies ran while one was open for 2% -> 2% of each run, Pallas kernels for 0% -> 0%
where the time goes in v1:
time: 395 us; the launch traced here: 394 us
  waiting for transfers between devices  191 us (48%)
  blocking collectives  118 us (30%)
  local copies, waits for them, and re-layouts  34.8 us (9%)
  matrix products  16.2 us (4%)
  between operations  13.6 us (3%)
  starting transfers between devices  10.7 us (3%)
  other arithmetic  10.4 us (3%)
    all_to_all x1, blocking collectives, on_device(): lax.all_to_all(outgoing, 'expert', split_axis=0, concat_axis=0, tiled=True)  77.4 us
    reduce_scatter x1, waiting for transfers between devices, on_device(): lax.psum_scatter(up_part, 'dp', scatter_dimension=3, tiled=True)  68.9 us
    all_to_all x1, waiting for transfers between devices, on_device(): lax.all_to_all(result, 'expert', split_axis=0, concat_axis=0, tiled=True)  65.1 us
    reduce_scatter x1, waiting for transfers between devices, on_device(): lax.psum_scatter(gate_part, 'dp', scatter_dimension=3, tiled=True)  56.6 us
    all_to_all x1, blocking collectives, on_device(): lax.all_to_all(jnp.stack([hidden] * lax.axis_size('dp')), 'dp', 0, 0)  40.4 us
    all_to_all x1, starting transfers between devices, on_device(): lax.all_to_all(result, 'expert', split_axis=0, concat_axis=0, tiled=True)  10.7 us
  transfers between devices with their start and end apart: 3, of which 3 were waited for; matrix products, arithmetic and copies ran while one was open for 2% of the time, Pallas kernels for 0%

profile of v1, /device:TPU:2, one launch (start us, length us, event | category | flops | bytes accessed | tf_op | source)
XLA Modules:
  0.0 394.1 jit_solution(8755753257736497043)
XLA Ops:
  6.5 0.8 copy.37
  8.1 0.7 add_multiply_fusion
  10.5 0.8 select_reduce_fusion
  11.5 4.3 %scatter_custom_fusion = s32[1536]{0:T(1024)S(1)} fusion(s32[1024]{0:T(1024)S(1)} %bitcast.39, s32[1024]{0:T(1024)S(1)} %iota.18, s32[]{:T(128)} %constant.20.clone.1), kind=kCustom, calls=%fused_computation.43 | custom fusion | bytes 6148 | tf_op jit(solution)/shard_map/scatter | solution.py:42
  15.9 5.1 %gather_fusion = bf16[1536,896]{1,0:T(8,128)(2,1)S(1)} fusion(bf16[128,896]{1,0:T(8,128)(2,1)S(1)} %copy-done, s32[2048]{0:T(1024)S(1)} %pad_clamp_fusion), kind=kCustom, calls=%fused_computation | custom fusion | bytes 5511168 | tf_op jit(solution)/shard_map/gather | solution.py:44
  21.0 2.5 gather.9
  23.6 2.4 broadcast_select_fusion
  26.0 2.2 copy.40
  28.2 77.4 %all_to_all.15 = bf16[64,2,12,896]{3,1,2,0:T(2,128)(2,1)S(1)} all-to-all(bf16[64,2,12,896]{3,1,2,0:T(2,128)(2,1)S(1)} %copy.40), channel_id=1, replica_groups=mesh['dp'=4,'expert'=64] {'expert'}, dimensions={0} | all-to-all | bytes 5505024 | tf_op jit(solution)/shard_map/all_to_all | solution.py:48
  105.6 5.3 %fusion.4 = f32[64,2,12,1024]{3,0,2,1:T(8,128)} fusion(bf16[64,2,12,896]{3,1,2,0:T(2,128)(2,1)S(1)} %all_to_all.15, bf16[1,2,896,1024]{3,2,1,0:T(8,128)(2,1)S(1)} %copy-done.3), kind=kOutput, calls=%fused_computation.10 | convolution fusion | flops 2818572288 | bytes 10878976 | tf_op jit(solution)/shard_map/nkcd,df->nkcf/dot_general | solution.py:49
  110.9 6.8 %fusion.2 = f32[64,2,12,1024]{3,0,2,1:T(8,128)} fusion(bf16[64,2,12,896]{3,1,2,0:T(2,128)(2,1)S(1)} %all_to_all.15, bf16[1,2,896,1024]{3,2,1,0:T(8,128)(2,1)} %param.16), kind=kOutput, calls=%fused_computation.8 | convolution fusion | flops 2818572288 | bytes 10878976 | tf_op jit(solution)/shard_map/nkcd,df->nkcf/dot_general | solution.py:50
  117.7 56.6 %reduce-scatter.3.cloned.1.call-done = f32[64,2,12,256]{3,0,2,1:T(8,128)} async-done(((f32[64,2,12,1024]{3,0,2,1:T(8,128)}), f32[64,2,12,256]{3,0,2,1:T(8,128)}) %reduce-scatter.3.cloned.1.call-update) | async-done | bytes 1572880 | tf_op jit(solution)/shard_map/reduce_scatter | solution.py:52
  174.3 68.9 %reduce-scatter.5.cloned.1.call-done = f32[64,2,12,256]{3,0,2,1:T(8,128)} async-done(((f32[64,2,12,1024]{3,0,2,1:T(8,128)}), f32[64,2,12,256]{3,0,2,1:T(8,128)}) %reduce-scatter.5.cloned.1.call-update) | async-done | bytes 1572880 | tf_op jit(solution)/shard_map/reduce_scatter | solution.py:53
  243.2 2.4 multiply_convert_fusion
  246.0 40.4 %all_to_all.16 = bf16[4,64,2,12,256]{4,1,3,2,0:T(8,128)(2,1)S(1)} all-to-all(bf16[4,64,2,12,256]{4,1,3,2,0:T(8,128)(2,1)S(1)} %stack.2), channel_id=1, replica_groups=mesh['dp'=4,'expert'=64] {'dp'}, dimensions={0} | all-to-all | bytes 6291456 | tf_op jit(solution)/shard_map/all_to_all | solution.py:57
  286.8 1.6 copy-done.4
  288.4 3.6 convolution_convert_fusion
  292.0 4.4 %copy.44 = bf16[64,2,12,896]{3,1,2,0:T(2,128)(2,1)} copy(bf16[64,2,12,896]{3,0,2,1:T(8,128)(2,1)S(1)} %convolution_convert_fusion) | data formatting | bytes 5505024 | tf_op jit(solution)/shard_map/convert_element_type | solution.py:60
  296.4 10.7 %all-to-all-start.2 = ((bf16[64,2,12,896]{3,1,2,0:T(2,128)(2,1)}), bf16[64,2,12,896]{3,1,2,0:T(2,128)(2,1)S(1)}, u32[]{:S(2)}, u32[]{:S(2)}) async-start(bf16[64,2,12,896]{3,1,2,0:T(2,128)(2,1)} %copy.44), calls=%async_computation.4 | async-start | bytes 5505024 | tf_op jit(solution)/shard_map/all_to_all | solution.py:61
  307.3 65.1 %all-to-all-done.2 = bf16[64,2,12,896]{3,1,2,0:T(2,128)(2,1)S(1)} async-done(((bf16[64,2,12,896]{3,1,2,0:T(2,128)(2,1)}), bf16[64,2,12,896]{3,1,2,0:T(2,128)(2,1)S(1)}, u32[]{:S(2)}, u32[]{:S(2)}) %all-to-all-start.2) | async-done | bytes 2752544 | tf_op jit(solution)/shard_map/all_to_all | solution.py:61
  372.4 2.4 copy.45
  374.8 3.8 reshape.144
  378.7 5.3 %gather_fusion.1 = bf16[1024,896]{1,0:T(8,128)(2,1)} fusion(bf16[1536,896]{1,0:T(8,128)(2,1)S(1)} %reshape.144, s32[1024]{0:T(1024)S(1)} %broadcast_clamp_fusion), kind=kCustom, calls=%fused_computation.1 | custom fusion | bytes 3674112 | tf_op jit(solution)/shard_map/gather | solution.py:63
  383.9 3.4 fusion.1
  (37 shorter events, 3.8 us)
Async XLA Ops:
  6.5 9.3 %copy-start = (bf16[128,896]{1,0:T(8,128)(2,1)S(1)}, bf16[128,896]{1,0:T(8,128)(2,1)}, u32[]{:S(2)}) copy-start(bf16[128,896]{1,0:T(8,128)(2,1)} %param.9) | copy-start | bytes 688132
  6.5 167.8 %reduce-scatter.3.cloned.1.call-start = ((), (), s32[]{:S(2)}) async-start(), calls=%async_computation.5 | async-start | bytes 7864320 | tf_op jit(solution)/shard_map/reduce_scatter | solution.py:52
  28.2 77.4 %copy-start.3 = (bf16[1,2,896,1024]{3,2,1,0:T(8,128)(2,1)S(1)}, bf16[1,2,896,1024]{3,2,1,0:T(8,128)(2,1)}, u32[]{:S(2)}) copy-start(bf16[1,2,896,1024]{3,2,1,0:T(8,128)(2,1)} %param.15) | copy-start | bytes 11010052
  110.9 132.3 %reduce-scatter.5.cloned.1.call-start = ((), (), s32[]{:S(2)}) async-start(), calls=%async_computation.6 | async-start | bytes 7864320 | tf_op jit(solution)/shard_map/reduce_scatter | solution.py:53
  286.4 2.0 copy-start.4
  296.4 10.8 %copy-start.2 = (f32[128,8]{0,1:T(8,128)S(1)}, f32[128,8]{0,1:T(8,128)}, u32[]{:S(2)}) copy-start(f32[128,8]{0,1:T(8,128)} %param.12) | copy-start | bytes 12292
  296.4 76.0 %all-to-all-start.2 = ((bf16[64,2,12,896]{3,1,2,0:T(2,128)(2,1)}), bf16[64,2,12,896]{3,1,2,0:T(2,128)(2,1)S(1)}, u32[]{:S(2)}, u32[]{:S(2)}) async-start(bf16[64,2,12,896]{3,1,2,0:T(2,128)(2,1)} %copy.44), calls=%async_computation.4 | async-start | bytes 5505024 | tf_op jit(solution)/shard_map/all_to_all | solution.py:61
  378.7 8.6 %copy-start.1 = (bf16[128,896]{1,0:T(8,128)(2,1)S(1)}, bf16[128,896]{1,0:T(8,128)(2,1)}, u32[]{:S(2)}) copy-start(bf16[128,896]{1,0:T(8,128)(2,1)} %param.9) | copy-start | bytes 688132
Sparse Core Ops, SparseCore 0:
  111.0 63.3 reduce-scatter.2
  176.9 66.2 reduce-scatter.4
